TPU v7x, 32 devices: a whole 2x2x4 slice. The times are simulated.
32 devices in a mesh: fsdp: 4 (over z), ctx: 4 (over x, core), tensor: 2 (over y).
Axes of the slice: x: 2, y: 2, z: 4, core: 2. Of those that a mesh axis runs over, the one named last changes fastest.
Arguments:
- tokens_in: bfloat16 [16384, 2048], P(('fsdp', 'ctx', 'tensor')), may hold values from -6 to 6
- attn_gain: float32 [2048], replicated, may hold values from 0.5 to 1.5
- query_weight: bfloat16 [2048, 2048], P('fsdp', 'tensor'), may hold values from -0.1875 to 0.1875
- key_weight: bfloat16 [2048, 2048], P('fsdp', 'tensor'), may hold values from -0.1875 to 0.1875
- value_weight: bfloat16 [2048, 2048], P('fsdp', 'tensor'), may hold values from -0.125 to 0.125
- output_weight: bfloat16 [2048, 2048], P('fsdp', 'tensor'), may hold values from -1 to 1
- mlp_gain: float32 [2048], replicated, may hold values from 0.5 to 1.5
- gate_weight: bfloat16 [2048, 8192], P('fsdp', 'tensor'), may hold values from -0.125 to 0.125
- up_weight: bfloat16 [2048, 8192], P('fsdp', 'tensor'), may hold values from -0.125 to 0.125
- down_weight: bfloat16 [2048, 8192], P('fsdp', 'tensor'), may hold values from -0.0625 to 0.0625
- seg_lengths: int32 [4, 20], P('fsdp'), may hold values from 1 to 128, 1920 in all within a row
- leaf_parent: int32 [4, 16], P('fsdp'), may hold values from 1 to 4
- cotangent: bfloat16 [16384, 2048], P(('fsdp', 'ctx', 'tensor')), may hold values from -6 to 6
Outputs:
- block_out: bfloat16 [16384, 2048], P(('fsdp', 'ctx', 'tensor'))
- input_grad: bfloat16 [16384, 2048], P(('fsdp', 'ctx', 'tensor'))
- attn_gain_grad: float32 [2048], P(('fsdp', 'ctx', 'tensor'))
- query_grad: float32 [2048, 2048], P(('fsdp', 'ctx'), 'tensor')
- key_grad: float32 [2048, 2048], P(('fsdp', 'ctx'), 'tensor')
- value_grad: float32 [2048, 2048], P(('fsdp', 'ctx'), 'tensor')
- output_grad: float32 [2048, 2048], P(('fsdp', 'ctx'), 'tensor')
- mlp_gain_grad: float32 [2048], P(('fsdp', 'ctx', 'tensor'))
- gate_grad: float32 [2048, 8192], P(('fsdp', 'ctx'), 'tensor')
- up_grad: float32 [2048, 8192], P(('fsdp', 'ctx'), 'tensor')
- down_grad: float32 [2048, 8192], P(('fsdp', 'ctx'), 'tensor')
Inputs may be any that keep to these rules, and one draw needn't show every extreme that they name: `seg_lengths`: row t gives the token counts of tree t's 4 branches and then its 16 leaves, which follow its trunk of 2176 tokens in this order; each row sums to 1920 and its largest entry is 128. `leaf_parent`: the branch, numbered 1 to 4, that each leaf hangs from.
All inputs are finite; a program needn't handle non-finite values.
Results may differ from a plain program's by a relative error of at most 0.02.
Values may be sent and summed in bfloat16 or wider, within the bound.
A program may use at most 448 MiB of HBM per device.

v0:
```python
import jax
import jax.numpy as jnp
from jax import lax
from jax.sharding import PartitionSpec as P

HEAD_DIM = 64
TRUNK = 2176
ROPE_BASE = 130000.0
EPSILON = 1e-05
NEG_LARGE = -1e30


def pick_table(onehot, table):
    return jnp.sum(jnp.where(onehot, table[None, :], 0), axis=1)


def tree_tables(lengths_row, parent_row, tree_len):
    branches = lengths_row.shape[0] - parent_row.shape[0]
    ends = TRUNK + jnp.cumsum(lengths_row)
    starts = ends - lengths_row
    matches = parent_row[:, None] - 1 == jnp.arange(branches, dtype=jnp.int32)[None, :]
    parent_len = jnp.sum(jnp.where(matches, lengths_row[None, :branches], 0), axis=1)
    zero_one = jnp.zeros((1,), jnp.int32)
    seg_start = jnp.concatenate([zero_one, starts])
    seg_base = jnp.concatenate(
        [zero_one, jnp.full((branches,), TRUNK, jnp.int32), TRUNK + parent_len]
    )
    seg_parent = jnp.concatenate([zero_one, jnp.zeros((branches,), jnp.int32), parent_row])
    positions = jnp.arange(tree_len, dtype=jnp.int32)
    above = jnp.sum((ends[None, :] <= positions[:, None]).astype(jnp.int32), axis=1)
    segment = (positions >= TRUNK).astype(jnp.int32) + above
    onehot = segment[:, None] == jnp.arange(seg_start.shape[0], dtype=jnp.int32)[None, :]
    depth = positions - pick_table(onehot, seg_start) + pick_table(onehot, seg_base)
    parent = pick_table(onehot, seg_parent)
    return (segment, parent, depth)


def rotate(values, depth, sign):
    count = values.shape[0]
    width = values.shape[1]
    heads = width // HEAD_DIM
    half = HEAD_DIM // 2
    freqs = jnp.power(ROPE_BASE, -(2.0 * jnp.arange(half, dtype=jnp.float32)) / HEAD_DIM)
    angles = depth.astype(jnp.float32)[:, None] * freqs[None, :]
    cosine = jnp.cos(angles)[:, None, :]
    sine = sign * jnp.sin(angles)[:, None, :]
    shaped = values.reshape(count, heads, HEAD_DIM)
    first = shaped[..., :half]
    second = shaped[..., half:]
    turned = jnp.concatenate(
        [first * cosine - second * sine, second * cosine + first * sine], axis=-1
    )
    return turned.reshape(count, width)


def normalize(rows):
    norm_inv = lax.rsqrt(jnp.mean(rows * rows, axis=1, keepdims=True) + EPSILON)
    return (rows * norm_inv, norm_inv)


def norm_backward(grad_rows, scaled, norm_inv, gain):
    weighted = grad_rows * gain[None, :]
    inner = jnp.mean(weighted * scaled, axis=1, keepdims=True)
    return (norm_inv * (weighted - scaled * inner), jnp.sum(grad_rows * scaled, axis=0))


def spread_rows(rows):
    return lax.all_gather(rows, "tensor", axis=0, tiled=True)


def reduce_rows(rows):
    return lax.psum_scatter(rows, "tensor", scatter_dimension=0, tiled=True)


def contract_first(left, right):
    return lax.dot_general(
        left, right, (((0,), (0,)), ((), ())), preferred_element_type=jnp.float32
    )


def contract_last(left, right):
    return lax.dot_general(
        left, right, (((1,), (1,)), ((), ())), preferred_element_type=jnp.float32
    )


def body(
    tokens_in,
    attn_gain,
    query_weight,
    key_weight,
    value_weight,
    output_weight,
    mlp_gain,
    gate_weight,
    up_weight,
    down_weight,
    seg_lengths,
    leaf_parent,
    cotangent,
):
    local_rows = tokens_in.shape[0]
    piece = local_rows * lax.axis_size("tensor")
    blocks = lax.axis_size("ctx")
    tree_len = piece * blocks
    score_scale = HEAD_DIM ** (-0.5)
    segment, parent, depth = tree_tables(seg_lengths[0], leaf_parent[0], tree_len)
    first_row = lax.axis_index("ctx") * piece
    query_seg = lax.dynamic_slice_in_dim(segment, first_row, piece)
    query_par = lax.dynamic_slice_in_dim(parent, first_row, piece)
    query_depth = lax.dynamic_slice_in_dim(depth, first_row, piece)
    query_index = first_row + jnp.arange(piece, dtype=jnp.int32)
    key_seg = segment.reshape(blocks, piece)
    key_index = jnp.arange(tree_len, dtype=jnp.int32).reshape(blocks, piece)
    wq_full, wk_full, wv_full, wo_full = (
        lax.all_gather(query_weight, "fsdp", axis=0, tiled=True),
        lax.all_gather(key_weight, "fsdp", axis=0, tiled=True),
        lax.all_gather(value_weight, "fsdp", axis=0, tiled=True),
        lax.all_gather(output_weight, "fsdp", axis=0, tiled=True),
    )
    wg_full, wu_full, wd_full = (
        lax.all_gather(gate_weight, "fsdp", axis=0, tiled=True),
        lax.all_gather(up_weight, "fsdp", axis=0, tiled=True),
        lax.all_gather(down_weight, "fsdp", axis=0, tiled=True),
    )
    x_rows = tokens_in.astype(jnp.float32)
    attn_scaled, attn_inv = normalize(x_rows)
    attn_in = spread_rows((attn_scaled * attn_gain[None, :]).astype(jnp.bfloat16))
    query_pre = jnp.dot(attn_in, wq_full, preferred_element_type=jnp.float32)
    key_pre = jnp.dot(attn_in, wk_full, preferred_element_type=jnp.float32)
    value_pre = jnp.dot(attn_in, wv_full, preferred_element_type=jnp.float32)
    query_rows = rotate(query_pre, query_depth, 1.0).astype(jnp.bfloat16)
    key_rows = rotate(key_pre, query_depth, 1.0).astype(jnp.bfloat16)
    value_rows = value_pre.astype(jnp.bfloat16)
    key_all, value_all = (
        lax.all_gather(key_rows, "ctx", axis=0, tiled=True),
        lax.all_gather(value_rows, "ctx", axis=0, tiled=True),
    )
    width = query_rows.shape[1]
    heads = width // HEAD_DIM
    query_heads = query_rows.reshape(piece, heads, HEAD_DIM)
    key_blocks = key_all.reshape(blocks, piece, heads, HEAD_DIM)
    value_blocks = value_all.reshape(blocks, piece, heads, HEAD_DIM)

    def block_scores(key_block, seg_block, index_block):
        raw = (
            jnp.einsum("qhd,khd->hqk", query_heads, key_block, preferred_element_type=jnp.float32)
            * score_scale
        )
        seen = (
            (seg_block[None, :] == query_seg[:, None])
            | (seg_block[None, :] == 0)
            | (seg_block[None, :] == query_par[:, None])
        ) & (index_block[None, :] <= query_index[:, None])
        return jnp.where(seen[None], raw, NEG_LARGE)

    def total_step(running, inputs):
        largest, total = running
        key_block, seg_block, index_block = inputs
        scores = block_scores(key_block, seg_block, index_block)
        newest = jnp.maximum(largest, jnp.max(scores, axis=2, keepdims=True))
        total = total * jnp.exp(largest - newest) + jnp.sum(
            jnp.exp(scores - newest), axis=2, keepdims=True
        )
        return ((newest, total), None)

    start_max = jnp.full((heads, piece, 1), NEG_LARGE, jnp.float32)
    start_total = jnp.zeros((heads, piece, 1), jnp.float32)
    (largest, total), unused = lax.scan(
        total_step, (start_max, start_total), (key_blocks, key_seg, key_index)
    )
    log_total = largest + jnp.log(total)

    def output_step(weighted, inputs):
        key_block, value_block, seg_block, index_block = inputs
        probs = jnp.exp(block_scores(key_block, seg_block, index_block) - log_total).astype(
            jnp.bfloat16
        )
        return (
            weighted
            + jnp.einsum("hqk,khd->qhd", probs, value_block, preferred_element_type=jnp.float32),
            None,
        )

    key_inputs = (key_blocks, value_blocks, key_seg, key_index)
    weighted, unused = lax.scan(
        output_step, jnp.zeros((piece, heads, HEAD_DIM), jnp.float32), key_inputs
    )
    attn_out = weighted.reshape(piece, width).astype(jnp.bfloat16)
    mid_rows = x_rows + reduce_rows(contract_last(attn_out, wo_full))
    mlp_scaled, mlp_inv = normalize(mid_rows)
    mlp_in = spread_rows((mlp_scaled * mlp_gain[None, :]).astype(jnp.bfloat16))
    gate = jnp.dot(mlp_in, wg_full, preferred_element_type=jnp.float32)
    up_proj = jnp.dot(mlp_in, wu_full, preferred_element_type=jnp.float32)
    hidden = (jax.nn.silu(gate) * up_proj).astype(jnp.bfloat16)
    final_rows = mid_rows + reduce_rows(contract_last(hidden, wd_full))
    block_out = final_rows.astype(jnp.bfloat16)
    out_grad_all = spread_rows(cotangent)
    down_grad = contract_first(out_grad_all, hidden)
    hidden_grad = jnp.dot(out_grad_all, wd_full, preferred_element_type=jnp.float32)
    sigmoid_gate = jax.nn.sigmoid(gate)
    gate_rows_grad = (
        hidden_grad * up_proj * sigmoid_gate * (1.0 + gate * (1.0 - sigmoid_gate))
    ).astype(jnp.bfloat16)
    up_rows_grad = (hidden_grad * gate * sigmoid_gate).astype(jnp.bfloat16)
    gate_grad = contract_first(mlp_in, gate_rows_grad)
    up_grad = contract_first(mlp_in, up_rows_grad)
    mlp_in_grad = reduce_rows(
        contract_last(gate_rows_grad, wg_full) + contract_last(up_rows_grad, wu_full)
    )
    mlp_back, mlp_gain_part = norm_backward(mlp_in_grad, mlp_scaled, mlp_inv, mlp_gain)
    mid_grad = cotangent.astype(jnp.float32) + mlp_back
    mid_all = spread_rows(mid_grad.astype(jnp.bfloat16))
    output_grad = contract_first(mid_all, attn_out)
    out_heads_grad = (
        jnp.dot(mid_all, wo_full, preferred_element_type=jnp.float32)
        .astype(jnp.bfloat16)
        .reshape(piece, heads, HEAD_DIM)
    )

    def delta_step(delta, inputs):
        key_block, value_block, seg_block, index_block = inputs
        attn_prob = jnp.exp(block_scores(key_block, seg_block, index_block) - log_total)
        prob_grad = jnp.einsum(
            "qhd,khd->hqk", out_heads_grad, value_block, preferred_element_type=jnp.float32
        )
        return (delta + jnp.sum(attn_prob * prob_grad, axis=2, keepdims=True), None)

    delta, unused = lax.scan(delta_step, jnp.zeros((heads, piece, 1), jnp.float32), key_inputs)

    def grad_step(query_total, inputs):
        key_block, value_block, seg_block, index_block = inputs
        attn_prob = jnp.exp(block_scores(key_block, seg_block, index_block) - log_total)
        prob_grad = jnp.einsum(
            "qhd,khd->hqk", out_heads_grad, value_block, preferred_element_type=jnp.float32
        )
        score_grad = (attn_prob * (prob_grad - delta)).astype(jnp.bfloat16)
        query_total = (
            query_total
            + jnp.einsum("hqk,khd->qhd", score_grad, key_block, preferred_element_type=jnp.float32)
            * score_scale
        )
        key_part = (
            jnp.einsum("hqk,qhd->khd", score_grad, query_heads, preferred_element_type=jnp.float32)
            * score_scale
        )
        value_part = jnp.einsum(
            "hqk,qhd->khd",
            attn_prob.astype(jnp.bfloat16),
            out_heads_grad,
            preferred_element_type=jnp.float32,
        )
        return (query_total, (key_part, value_part))

    query_sum, (key_parts, value_parts) = lax.scan(
        grad_step, jnp.zeros((piece, heads, HEAD_DIM), jnp.float32), key_inputs
    )
    key_sum, value_sum = (
        lax.psum_scatter(
            key_parts.reshape(tree_len, width).astype(jnp.bfloat16),
            "ctx",
            scatter_dimension=0,
            tiled=True,
        ).astype(jnp.float32),
        lax.psum_scatter(
            value_parts.reshape(tree_len, width).astype(jnp.bfloat16),
            "ctx",
            scatter_dimension=0,
            tiled=True,
        ).astype(jnp.float32),
    )
    query_pre_grad = rotate(query_sum.reshape(piece, width), query_depth, -1.0).astype(jnp.bfloat16)
    key_pre_grad = rotate(key_sum, query_depth, -1.0).astype(jnp.bfloat16)
    value_pre_grad = value_sum.astype(jnp.bfloat16)
    query_grad = contract_first(attn_in, query_pre_grad)
    key_grad = contract_first(attn_in, key_pre_grad)
    value_grad = contract_first(attn_in, value_pre_grad)
    attn_in_grad = reduce_rows(
        contract_last(query_pre_grad, wq_full)
        + contract_last(key_pre_grad, wk_full)
        + contract_last(value_pre_grad, wv_full)
    )
    attn_back, attn_gain_part = norm_backward(attn_in_grad, attn_scaled, attn_inv, attn_gain)
    input_grad = (mid_grad + attn_back).astype(jnp.bfloat16)
    attn_gain_grad, mlp_gain_grad = (
        lax.psum_scatter(
            attn_gain_part, ("fsdp", "ctx", "tensor"), scatter_dimension=0, tiled=True
        ),
        lax.psum_scatter(mlp_gain_part, ("fsdp", "ctx", "tensor"), scatter_dimension=0, tiled=True),
    )
    query_out, key_out, value_out, output_out, gate_out, up_out, down_out = (
        lax.psum_scatter(
            query_grad.astype(jnp.bfloat16), ("fsdp", "ctx"), scatter_dimension=0, tiled=True
        ).astype(jnp.float32),
        lax.psum_scatter(
            key_grad.astype(jnp.bfloat16), ("fsdp", "ctx"), scatter_dimension=0, tiled=True
        ).astype(jnp.float32),
        lax.psum_scatter(
            value_grad.astype(jnp.bfloat16), ("fsdp", "ctx"), scatter_dimension=0, tiled=True
        ).astype(jnp.float32),
        lax.psum_scatter(
            output_grad.astype(jnp.bfloat16), ("fsdp", "ctx"), scatter_dimension=0, tiled=True
        ).astype(jnp.float32),
        lax.psum_scatter(
            gate_grad.astype(jnp.bfloat16), ("fsdp", "ctx"), scatter_dimension=0, tiled=True
        ).astype(jnp.float32),
        lax.psum_scatter(
            up_grad.astype(jnp.bfloat16), ("fsdp", "ctx"), scatter_dimension=0, tiled=True
        ).astype(jnp.float32),
        lax.psum_scatter(
            down_grad.astype(jnp.bfloat16), ("fsdp", "ctx"), scatter_dimension=0, tiled=True
        ).astype(jnp.float32),
    )
    return (
        block_out,
        input_grad,
        attn_gain_grad,
        query_out,
        key_out,
        value_out,
        output_out,
        mlp_gain_grad,
        gate_out,
        up_out,
        down_out,
    )


def solution(mesh):
    in_specs = (
        P(("fsdp", "ctx", "tensor"), None),
        P(),
        P("fsdp", "tensor"),
        P("fsdp", "tensor"),
        P("fsdp", "tensor"),
        P("fsdp", "tensor"),
        P(),
        P("fsdp", "tensor"),
        P("fsdp", "tensor"),
        P("fsdp", "tensor"),
        P("fsdp", None),
        P("fsdp", None),
        P(("fsdp", "ctx", "tensor"), None),
    )
    out_specs = (
        P(("fsdp", "ctx", "tensor"), None),
        P(("fsdp", "ctx", "tensor"), None),
        P(("fsdp", "ctx", "tensor")),
        P(("fsdp", "ctx"), "tensor"),
        P(("fsdp", "ctx"), "tensor"),
        P(("fsdp", "ctx"), "tensor"),
        P(("fsdp", "ctx"), "tensor"),
        P(("fsdp", "ctx", "tensor")),
        P(("fsdp", "ctx"), "tensor"),
        P(("fsdp", "ctx"), "tensor"),
        P(("fsdp", "ctx"), "tensor"),
    )
    return jax.shard_map(body, mesh=mesh, in_specs=in_specs, out_specs=out_specs, check_vma=False)
```

profile of v0, /device:TPU:0, one launch (start us, length us, event | category | flops | bytes accessed | tf_op | source)
XLA Modules:
  0.0 4075.0 jit_solution(14927405452069166986)
XLA Ops:
  17.7 55.3 %all-gather.14.cloned.1.call-done = bf16[1024,2048]{1,0:T(8,128)(2,1)} async-done(((bf16[512,2048]{1,0:T(8,128)(2,1)}), bf16[1024,2048]{1,0:T(8,128)(2,1)}) %all-gather.14.cloned.1.call-update) | async-done | bytes 4194320 | tf_op jit(solution)/shard_map/all_gather | solution.py:68
  73.0 82.4 %all-gather.24.cloned.1.call-done = bf16[2048,1024]{1,0:T(8,128)(2,1)} async-done(((bf16[512,1024]{1,0:T(8,128)(2,1)}), bf16[2048,1024]{1,0:T(8,128)(2,1)}) %all-gather.24.cloned.1.call-update) | async-done | bytes 4194320 | tf_op jit(solution)/shard_map/all_gather | solution.py:116
  165.4 70.9 %all-gather.20.cloned.1.call-done = bf16[2048,1024]{1,0:T(8,128)(2,1)} async-done(((bf16[512,1024]{1,0:T(8,128)(2,1)}), bf16[2048,1024]{1,0:T(8,128)(2,1)}) %all-gather.20.cloned.1.call-update) | async-done | bytes 4194320 | tf_op jit(solution)/shard_map/all_gather | solution.py:117
  248.3 68.8 %all-gather.16.cloned.1.call-done = bf16[2048,1024]{1,0:T(8,128)(2,1)} async-done(((bf16[512,1024]{1,0:T(8,128)(2,1)}), bf16[2048,1024]{1,0:T(8,128)(2,1)}) %all-gather.16.cloned.1.call-update) | async-done | bytes 4194320 | tf_op jit(solution)/shard_map/all_gather | solution.py:118
  400.2 197.2 %while.50 = (s32[]{:T(128)}, f32[16,1024,1]{1,0,2:T(8,128)S(1)}, f32[16,1024,1]{1,0,2:T(8,128)S(1)}, s32[4,1024]{1,0:T(4,128)S(1)}, s32[1024]{0:T(1024)S(1)}, /*...) while((s32[]{:T(128)}, f32[16,1024,1]{1,0,2:T(8,128)S(1)}, ...), condition=%wide.region_10.11_spmd.clone, body=%wide.region_7.10_spmd.clone.sunk | while | flops 2271299584 | bytes 142452880 | solution.py:169
  637.9 109.1 %while.51 = (s32[]{:T(128)}, f32[1024,16,64]{0,2,1:T(8,128)}, bf16[4,1024,16,64]{1,3,2,0:T(8,128)(2,1)}, s32[4,1024]{1,0:T(4,128)S(1)}, s32[1024]{0:T(1024)S(1)}...) while((s32[]{:T(128)}, f32[1024,16,64]{0,2,1:T(8,128)}, ...), condition=%wide.region_12.13_spmd.clone, body=%wide.region_11.12_spmd.clone.sunk | while | flops 4370466816 | bytes 16887448 | solution.py:186
  763.2 98.6 %reduce-scatter.16.cloned.1.call-done = f32[512,2048]{1,0:T(8,128)} async-done(((f32[1024,2048]{1,0:T(8,128)}), f32[512,2048]{1,0:T(8,128)}) %reduce-scatter.16.cloned.1.call-update) | async-done | bytes 4194320 | tf_op jit(solution)/shard_map/reduce_scatter | solution.py:72
  870.4 279.8 %all-gather.32.cloned.1.call-done = bf16[2048,4096]{1,0:T(8,128)(2,1)} async-done(((bf16[512,4096]{1,0:T(8,128)(2,1)}), bf16[2048,4096]{1,0:T(8,128)(2,1)}) %all-gather.32.cloned.1.call-update) | async-done | bytes 16777232 | tf_op jit(solution)/shard_map/all_gather | solution.py:123
  1150.2 57.0 %all-gather.28.cloned.1.call-done = bf16[1024,2048]{1,0:T(8,128)(2,1)} async-done(((bf16[512,2048]{1,0:T(8,128)(2,1)}), bf16[1024,2048]{1,0:T(8,128)(2,1)}) %all-gather.28.cloned.1.call-update) | async-done | bytes 4194320 | tf_op jit(solution)/shard_map/all_gather | solution.py:68
  1230.6 265.0 %all-gather.30.cloned.1.call-done = bf16[2048,4096]{1,0:T(8,128)(2,1)} async-done(((bf16[512,4096]{1,0:T(8,128)(2,1)}), bf16[2048,4096]{1,0:T(8,128)(2,1)}) %all-gather.30.cloned.1.call-update) | async-done | bytes 16777232 | tf_op jit(solution)/shard_map/all_gather | solution.py:122
  1552.1 288.5 %all-gather.34.cloned.1.call-done = bf16[2048,4096]{1,0:T(8,128)(2,1)} async-done(((bf16[512,4096]{1,0:T(8,128)(2,1)}), bf16[2048,4096]{1,0:T(8,128)(2,1)}) %all-gather.34.cloned.1.call-update) | async-done | bytes 16777232 | tf_op jit(solution)/shard_map/all_gather | solution.py:124
  1919.1 97.5 %reduce-scatter.20.cloned.1.call-done = f32[512,2048]{1,0:T(8,128)} async-done(((f32[1024,2048]{1,0:T(8,128)}), f32[512,2048]{1,0:T(8,128)}) %reduce-scatter.20.cloned.1.call-update) | async-done | bytes 4194320 | tf_op jit(solution)/shard_map/reduce_scatter | solution.py:72
  2025.7 56.3 %all-gather.38.cloned.1.call-done = bf16[1024,2048]{1,0:T(8,128)(2,1)} async-done(((bf16[512,2048]{1,0:T(8,128)(2,1)}), bf16[1024,2048]{1,0:T(8,128)(2,1)}) %all-gather.38.cloned.1.call-update) | async-done | bytes 4194320 | tf_op jit(solution)/shard_map/all_gather | solution.py:68
  2091.4 223.1 %while.52 = (s32[]{:T(128)}, f32[16,1024,1]{1,2,0:T(1,128)S(1)}, s32[4,1024]{1,0:T(4,128)S(1)}, s32[1024]{0:T(1024)S(1)}, s32[1024]{0:T(1024)S(1)}, /*index=5*/s...) while((s32[]{:T(128)}, f32[16,1024,1]{1,2,0:T(1,128)S(1)}, ...), condition=%wide.region_20.21_spmd.clone, body=%wide.region_18.20_spmd.clone.sunk | while | flops 4385163264 | bytes 145074336 | solution.py:229
  2314.5 522.7 %while.53 = (s32[]{:T(128)}, f32[1024,16,64]{0,2,1:T(8,128)}, bf16[4,1024,16,64]{1,3,2,0:T(8,128)(2,1)}, bf16[4,1024,16,64]{1,3,2,0:T(8,128)(2,1)}, bf16[4,1024,...) while((s32[]{:T(128)}, f32[1024,16,64]{0,2,1:T(8,128)}, ...), condition=%wide.region_22.23_spmd.clone, body=%wide.region_21.22_spmd.clone.sunk | while | flops 10915678208 | bytes 336832672 | solution.py:255
  3084.9 104.4 %reduce-scatter.40.cloned.1.call-done = bf16[128,4096]{1,0:T(8,128)(2,1)} async-done(((bf16[2048,4096]{1,0:T(8,128)(2,1)}), bf16[128,4096]{1,0:T(8,128)(2,1)}) %reduce-scatter.40.cloned.1.call-update) | async-done | bytes 1048592
  3192.5 178.4 %reduce-scatter.38.cloned.1.call-done = bf16[128,4096]{1,0:T(8,128)(2,1)} async-done(((bf16[2048,4096]{1,0:T(8,128)(2,1)}), bf16[128,4096]{1,0:T(8,128)(2,1)}) %reduce-scatter.38.cloned.1.call-update) | async-done | bytes 1048592 | tf_op jit(solution)/shard_map/reduce_scatter | solution.py:307
  3373.7 178.8 %reduce-scatter.36.cloned.1.call-done = bf16[128,4096]{1,0:T(8,128)(2,1)} async-done(((bf16[2048,4096]{1,0:T(8,128)(2,1)}), bf16[128,4096]{1,0:T(8,128)(2,1)}) %reduce-scatter.36.cloned.1.call-update) | async-done | bytes 1048592 | tf_op jit(solution)/shard_map/reduce_scatter | solution.py:304
  3555.2 72.5 %reduce-scatter.34.cloned.1.call-done = bf16[128,1024]{1,0:T(8,128)(2,1)} async-done(((bf16[2048,1024]{1,0:T(8,128)(2,1)}), bf16[128,1024]{1,0:T(8,128)(2,1)}) %reduce-scatter.34.cloned.1.call-update) | async-done | bytes 262160 | tf_op jit(solution)/shard_map/reduce_scatter | solution.py:301
  3629.5 74.1 %reduce-scatter.32.cloned.1.call-done = bf16[128,1024]{1,0:T(8,128)(2,1)} async-done(((bf16[2048,1024]{1,0:T(8,128)(2,1)}), bf16[128,1024]{1,0:T(8,128)(2,1)}) %reduce-scatter.32.cloned.1.call-update) | async-done | bytes 262160 | tf_op jit(solution)/shard_map/reduce_scatter | solution.py:298
  3705.4 73.8 %reduce-scatter.28.cloned.1.call-done = bf16[128,1024]{1,0:T(8,128)(2,1)} async-done(((bf16[2048,1024]{1,0:T(8,128)(2,1)}), bf16[128,1024]{1,0:T(8,128)(2,1)}) %reduce-scatter.28.cloned.1.call-update) | async-done | bytes 262160 | tf_op jit(solution)/shard_map/reduce_scatter | solution.py:292
  3780.9 73.8 %reduce-scatter.30.cloned.1.call-done = bf16[128,1024]{1,0:T(8,128)(2,1)} async-done(((bf16[2048,1024]{1,0:T(8,128)(2,1)}), bf16[128,1024]{1,0:T(8,128)(2,1)}) %reduce-scatter.30.cloned.1.call-update) | async-done | bytes 262160 | tf_op jit(solution)/shard_map/reduce_scatter | solution.py:295
  3856.6 98.9 %reduce-scatter.26.cloned.1.call-done = f32[512,2048]{1,0:T(8,128)} async-done(((f32[1024,2048]{1,0:T(8,128)}), f32[512,2048]{1,0:T(8,128)}) %reduce-scatter.26.cloned.1.call-update) | async-done | bytes 4194320 | tf_op jit(solution)/shard_map/reduce_scatter | solution.py:72
  4000.0 58.3 %reduce-scatter.18.cloned.1.call-done = f32[512,2048]{1,0:T(8,128)} async-done(((f32[1024,2048]{1,0:T(8,128)}), f32[512,2048]{1,0:T(8,128)}) %reduce-scatter.18.cloned.1.call-update) | async-done | bytes 4194320 | tf_op jit(solution)/shard_map/reduce_scatter | solution.py:72
  (367 shorter events, 1725.3 us)
Async XLA Ops:
  14.2 222.1 %all-gather.20.cloned.1.call-start = ((), (), s32[]{:S(2)}) async-start(), calls=%async_computation.16 | async-start | bytes 5242880 | tf_op jit(solution)/shard_map/all_gather | solution.py:117
  14.9 302.1 %all-gather.16.cloned.1.call-start = ((), (), s32[]{:S(2)}) async-start(), calls=%async_computation.14 | async-start | bytes 5242880 | tf_op jit(solution)/shard_map/all_gather | solution.py:118
  15.5 360.4 %all-gather.22.cloned.1.call-start = ((), (), s32[]{:S(2)}) async-start(), calls=%async_computation.17 | async-start | bytes 10485760 | tf_op jit(solution)/shard_map/all_gather | solution.py:136
  248.0 349.4 %all-gather.18.cloned.1.call-start = ((), (), s32[]{:S(2)}) async-start(), calls=%async_computation.15 | async-start | bytes 10485760 | tf_op jit(solution)/shard_map/all_gather | solution.py:137
  326.3 425.3 %all-gather.26.cloned.1.call-start = ((), (), s32[]{:S(2)}) async-start(), calls=%async_computation.19 | async-start | bytes 5242880 | tf_op jit(solution)/shard_map/all_gather | solution.py:119
  327.1 534.6 %reduce-scatter.16.cloned.1.call-start = ((), (), s32[]{:S(2)}) async-start(), calls=%async_computation.20 | async-start | bytes 12582912 | tf_op jit(solution)/shard_map/reduce_scatter | solution.py:72
  762.4 387.8 %all-gather.32.cloned.1.call-start = ((), (), s32[]{:S(2)}) async-start(), calls=%async_computation.23 | async-start | bytes 20971520 | tf_op jit(solution)/shard_map/all_gather | solution.py:123
  763.1 444.1 %all-gather.28.cloned.1.call-start = ((), (), s32[]{:S(2)}) async-start(), calls=%async_computation.21 | async-start | bytes 6291456 | tf_op jit(solution)/shard_map/all_gather | solution.py:68
  868.3 627.4 %all-gather.30.cloned.1.call-start = ((), (), s32[]{:S(2)}) async-start(), calls=%async_computation.22 | async-start | bytes 20971520 | tf_op jit(solution)/shard_map/all_gather | solution.py:122
  869.0 683.1 %all-gather.36.cloned.1.call-start = ((), (), s32[]{:S(2)}) async-start(), calls=%async_computation.26 | async-start | bytes 6291456 | tf_op jit(solution)/shard_map/all_gather | solution.py:68
  869.6 971.0 %all-gather.34.cloned.1.call-start = ((), (), s32[]{:S(2)}) async-start(), calls=%async_computation.24 | async-start | bytes 20971520 | tf_op jit(solution)/shard_map/all_gather | solution.py:124
  870.4 1146.3 %reduce-scatter.20.cloned.1.call-start = ((), (), s32[]{:S(2)}) async-start(), calls=%async_computation.27 | async-start | bytes 12582912 | tf_op jit(solution)/shard_map/reduce_scatter | solution.py:72
  1919.1 162.9 %all-gather.38.cloned.1.call-start = ((), (), s32[]{:S(2)}) async-start(), calls=%async_computation.28 | async-start | bytes 6291456 | tf_op jit(solution)/shard_map/all_gather | solution.py:68
  2025.1 967.3 %reduce-scatter.24.cloned.1.call-start = ((), (), s32[]{:S(2)}) async-start(), calls=%async_computation.30 | async-start | bytes 10485760 | tf_op jit(solution)/shard_map/reduce_scatter | solution.py:265
  2860.4 146.2 %reduce-scatter.22.cloned.1.call-start = ((), (), s32[]{:S(2)}) async-start(), calls=%async_computation.29 | async-start | bytes 10485760 | tf_op jit(solution)/shard_map/reduce_scatter | solution.py:259
  2885.5 303.8 %reduce-scatter.40.cloned.1.call-start = ((), (), s32[]{:S(2)}) async-start(), calls=%async_computation.38 | async-start | bytes 17825792
  2931.0 439.9 %reduce-scatter.38.cloned.1.call-start = ((), (), s32[]{:S(2)}) async-start(), calls=%async_computation.37 | async-start | bytes 17825792 | tf_op jit(solution)/shard_map/reduce_scatter | solution.py:307
  2956.0 596.4 %reduce-scatter.36.cloned.1.call-start = ((), (), s32[]{:S(2)}) async-start(), calls=%async_computation.36 | async-start | bytes 17825792 | tf_op jit(solution)/shard_map/reduce_scatter | solution.py:304
  2981.9 645.8 %reduce-scatter.34.cloned.1.call-start = ((), (), s32[]{:S(2)}) async-start(), calls=%async_computation.35 | async-start | bytes 4456448 | tf_op jit(solution)/shard_map/reduce_scatter | solution.py:301
  2992.1 711.5 %reduce-scatter.32.cloned.1.call-start = ((), (), s32[]{:S(2)}) async-start(), calls=%async_computation.34 | async-start | bytes 4456448 | tf_op jit(solution)/shard_map/reduce_scatter | solution.py:298
  3001.8 777.3 %reduce-scatter.28.cloned.1.call-start = ((), (), s32[]{:S(2)}) async-start(), calls=%async_computation.32 | async-start | bytes 4456448 | tf_op jit(solution)/shard_map/reduce_scatter | solution.py:292
  3020.3 834.4 %reduce-scatter.30.cloned.1.call-start = ((), (), s32[]{:S(2)}) async-start(), calls=%async_computation.33 | async-start | bytes 4456448 | tf_op jit(solution)/shard_map/reduce_scatter | solution.py:295
  3030.6 924.9 %reduce-scatter.26.cloned.1.call-start = ((), (), s32[]{:S(2)}) async-start(), calls=%async_computation.31 | async-start | bytes 12582912 | tf_op jit(solution)/shard_map/reduce_scatter | solution.py:72
  3060.3 998.0 %reduce-scatter.18.cloned.1.call-start = ((), (), s32[]{:S(2)}) async-start(), calls=%async_computation.25 | async-start | bytes 12582912 | tf_op jit(solution)/shard_map/reduce_scatter | solution.py:72
  (51 other events, 5770.5 us)
Sparse Core Ops, SparseCore 0:
  13.5 59.4 all-gather.13
  74.6 80.7 all-gather.23
  157.0 79.2 all-gather.19
  237.7 79.2 all-gather.15
  319.0 56.8 all-gather.21
  377.9 58.2 all-gather.17
  437.7 80.7 all-gather.25
  762.5 99.2 reduce-scatter.15
  863.4 286.7 all-gather.31
  1208.9 286.7 all-gather.29
  1553.8 286.7 all-gather.33
  1919.2 97.4 reduce-scatter.19
  2025.2 56.7 all-gather.37
  2860.6 71.7 reduce-scatter.23
  2934.9 71.6 reduce-scatter.21
  3010.6 178.5 reduce-scatter.39
  3193.3 177.5 reduce-scatter.37
  3374.9 177.5 reduce-scatter.35
  3556.3 71.3 reduce-scatter.33
  3632.0 71.5 reduce-scatter.31
  3707.4 71.6 reduce-scatter.27
  3783.3 71.3 reduce-scatter.29
  3857.1 98.3 reduce-scatter.25
  3957.7 100.4 reduce-scatter.17
  (2 shorter events, 109.7 us)
where the time goes:
time: 4090 us; the launch traced here: 4070 us
  waiting for transfers between devices  2420 us (59%)
  matrix products  1260 us (31%)
  other arithmetic  179 us (4%)
  local copies, waits for them, and re-layouts  150 us (4%)
    reduce_scatter x4, waiting for transfers between devices, reduce_rows(): return lax.psum_scatter(rows, 'tensor', scatter_dimension=0, tiled=True)  353 us
    dot_general x12, matrix products, block_scores(): jnp.einsum('qhd,khd->hqk', query_heads, key_block, preferred_element_type...  300 us
    all_gather x1, waiting for transfers between devices, body(): lax.all_gather(down_weight, 'fsdp', axis=0, tiled=True)  288 us
    all_gather x1, waiting for transfers between devices, body(): lax.all_gather(up_weight, 'fsdp', axis=0, tiled=True)  280 us
    all_gather x1, waiting for transfers between devices, body(): lax.all_gather(gate_weight, 'fsdp', axis=0, tiled=True)  265 us
    all_gather x4, waiting for transfers between devices, spread_rows(): return lax.all_gather(rows, 'tensor', axis=0, tiled=True)  202 us
    reduce_scatter x1, waiting for transfers between devices, body(): lax.psum_scatter(gate_grad.astype(jnp.bfloat16), ('fsdp', 'ctx'), scatter...  179 us
    reduce_scatter x1, waiting for transfers between devices, body(): lax.psum_scatter(up_grad.astype(jnp.bfloat16), ('fsdp', 'ctx'), scatter_d...  178 us
  transfers between devices with their start and end apart: 26, of which 23 were waited for; matrix products, arithmetic and copies ran while one was open for 17% of the time, Pallas kernels for 0%

commit v1 on v0

--- a/solution.py
+++ b/solution.py
@@ -8,6 +8,24 @@
 ROPE_BASE = 130000.0
 EPSILON = 1e-05
 NEG_LARGE = -1e30
+
+
+def gather_around(array, axis, dim):
+    ways, here, step = (lax.axis_size(axis), lax.axis_index(axis), array.shape[dim])
+    dims = [n * ways if d == dim else n for d, n in enumerate(array.shape)]
+    full = lax.dynamic_update_slice_in_dim(
+        jnp.zeros(dims, array.dtype), array, here * step, axis=dim
+    )
+    going_up = going_down = array
+    for far in range(1, ways // 2 + 1):
+        going_up = lax.ppermute(going_up, axis, [(d, (d + 1) % ways) for d in range(ways)])
+        full = lax.dynamic_update_slice_in_dim(full, going_up, (here - far) % ways * step, axis=dim)
+        if 2 * far < ways:
+            going_down = lax.ppermute(going_down, axis, [(d, (d - 1) % ways) for d in range(ways)])
+            full = lax.dynamic_update_slice_in_dim(
+                full, going_down, (here + far) % ways * step, axis=dim
+            )
+    return full
 
 
 def pick_table(onehot, table):
@@ -119,7 +137,7 @@
         lax.all_gather(output_weight, "fsdp", axis=0, tiled=True),
     )
     wg_full, wu_full, wd_full = (
-        lax.all_gather(gate_weight, "fsdp", axis=0, tiled=True),
+        gather_around(gate_weight, "fsdp", 0),
         lax.all_gather(up_weight, "fsdp", axis=0, tiled=True),
         lax.all_gather(down_weight, "fsdp", axis=0, tiled=True),
     )

time: 4090 us -> 3930 us (0.961)
  waiting for transfers between devices: 2420 us -> 2230 us
    ppermute x0 -> x3, waiting for transfers between devices: none -> 346 us  [the longest x2 243 us: gather_around(): lax.ppermute(going_up, axis, [(d, (d + 1) % ways) for d in range(ways)])]
    all_gather x1 -> x0, waiting for transfers between devices: 265 us -> none  [body(): lax.all_gather(gate_weight, 'fsdp', axis=0, tiled=True)]
    all_gather x1, waiting for transfers between devices: 288 us -> 164 us  [body(): lax.all_gather(down_weight, 'fsdp', axis=0, tiled=True)]
    reduce_scatter x4, waiting for transfers between devices: 353 us -> 256 us  [reduce_rows(): return lax.psum_scatter(rows, 'tensor', scatter_dimension=0, tiled=True)]
    unnamed x27 -> x26, waiting for transfers between devices: 110 us -> 109 us
    unnamed x106 -> x110, local copies, waits for them, and re-layouts: 90.7 us -> 90.7 us
  transfers between devices with their start and end apart: 26 -> 28, of which waited for: 23 -> 23; matrix products, arithmetic and copies ran while one was open for 17% -> 18% of each run, Pallas kernels for 0% -> 0%
where the time goes in v1:
time: 3930 us; the launch traced here: 3920 us
  waiting for transfers between devices  2230 us (57%)
  matrix products  1270 us (32%)
  other arithmetic  179 us (5%)
  local copies, waits for them, and re-layouts  174 us (4%)
  blocking collectives  40.1 us (1%)
    dot_general x12, matrix products, block_scores(): jnp.einsum('qhd,khd->hqk', query_heads, key_block, preferred_element_type...  300 us
    all_gather x1, waiting for transfers between devices, body(): lax.all_gather(up_weight, 'fsdp', axis=0, tiled=True)  263 us
    reduce_scatter x4, waiting for transfers between devices, reduce_rows(): return lax.psum_scatter(rows, 'tensor', scatter_dimension=0, tiled=True)  256 us
    ppermute x2, waiting for transfers between devices, gather_around(): lax.ppermute(going_up, axis, [(d, (d + 1) % ways) for d in range(ways)])  243 us
    reduce_scatter x1, waiting for transfers between devices, body(): lax.psum_scatter(up_grad.astype(jnp.bfloat16), ('fsdp', 'ctx'), scatter_d...  179 us
    reduce_scatter x1, waiting for transfers between devices, body(): lax.psum_scatter(gate_grad.astype(jnp.bfloat16), ('fsdp', 'ctx'), scatter...  178 us
    all_gather x4, waiting for transfers between devices, spread_rows(): return lax.all_gather(rows, 'tensor', axis=0, tiled=True)  169 us
    dot_general x4, matrix products, grad_step(): jnp.einsum('qhd,khd->hqk', out_heads_grad, value_block, preferred_element...  165 us
  transfers between devices with their start and end apart: 28, of which 23 were waited for; matrix products, arithmetic and copies ran while one was open for 18% of the time, Pallas kernels for 0%

profile of v1, /device:TPU:0, one launch (start us, length us, event | category | flops | bytes accessed | tf_op | source)
XLA Modules:
  0.0 3915.2 jit_solution(10396700462037421087)
XLA Ops:
  73.0 82.4 %all-gather.23.cloned.1.call-done = bf16[2048,1024]{1,0:T(8,128)(2,1)} async-done(((bf16[512,1024]{1,0:T(8,128)(2,1)}), bf16[2048,1024]{1,0:T(8,128)(2,1)}) %all-gather.23.cloned.1.call-update) | async-done | bytes 4194320 | tf_op jit(solution)/shard_map/all_gather | solution.py:134
  165.3 70.9 %all-gather.19.cloned.1.call-done = bf16[2048,1024]{1,0:T(8,128)(2,1)} async-done(((bf16[512,1024]{1,0:T(8,128)(2,1)}), bf16[2048,1024]{1,0:T(8,128)(2,1)}) %all-gather.19.cloned.1.call-update) | async-done | bytes 4194320 | tf_op jit(solution)/shard_map/all_gather | solution.py:135
  248.5 68.5 %all-gather.15.cloned.1.call-done = bf16[2048,1024]{1,0:T(8,128)(2,1)} async-done(((bf16[512,1024]{1,0:T(8,128)(2,1)}), bf16[2048,1024]{1,0:T(8,128)(2,1)}) %all-gather.15.cloned.1.call-update) | async-done | bytes 4194320 | tf_op jit(solution)/shard_map/all_gather | solution.py:136
  400.2 197.1 %while.50 = (s32[]{:T(128)}, f32[16,1024,1]{1,0,2:T(8,128)S(1)}, f32[16,1024,1]{1,0,2:T(8,128)S(1)}, s32[4,1024]{1,0:T(4,128)S(1)}, s32[1024]{0:T(1024)S(1)}, /*...) while((s32[]{:T(128)}, f32[16,1024,1]{1,0,2:T(8,128)S(1)}, ...), condition=%wide.region_10.11_spmd.clone, body=%wide.region_7.10_spmd.clone.sunk | while | flops 2271299584 | bytes 142452880 | solution.py:187
  637.9 108.8 %while.51 = (s32[]{:T(128)}, f32[1024,16,64]{0,2,1:T(8,128)}, bf16[4,1024,16,64]{1,3,2,0:T(8,128)(2,1)}, s32[4,1024]{1,0:T(4,128)S(1)}, s32[1024]{0:T(1024)S(1)}...) while((s32[]{:T(128)}, f32[1024,16,64]{0,2,1:T(8,128)}, ...), condition=%wide.region_12.13_spmd.clone, body=%wide.region_11.12_spmd.clone.sunk | while | flops 4370466816 | bytes 16887448 | solution.py:204
  768.0 91.7 %collective-permute-done = bf16[512,4096]{1,0:T(8,128)(2,1)} collective-permute-done((bf16[512,4096]{1,0:T(8,128)(2,1)}, bf16[512,4096]{1,0:T(8,128)(2,1)}, u32[]{:S(2)}, u32[]{:S(2)}) %collective-permute-start) | collective-permute-done | bytes 4194336 | tf_op jit(solution)/shard_map/ppermute | solution.py:21
  881.1 103.8 %collective-permute-done.1 = bf16[512,4096]{1,0:T(8,128)(2,1)} collective-permute-done((bf16[512,4096]{1,0:T(8,128)(2,1)}, bf16[512,4096]{1,0:T(8,128)(2,1)}, u32[]{:S(2)}, u32[]{:S(2)}) %collective-permute-start.1) | collective-permute-done | bytes 4194336 | tf_op jit(solution)/shard_map/ppermute | solution.py:24
  989.7 150.8 %collective-permute-done.2 = bf16[512,4096]{1,0:T(8,128)(2,1)} collective-permute-done((bf16[512,4096]{1,0:T(8,128)(2,1)}, bf16[512,4096]{1,0:T(8,128)(2,1)}, u32[]{:S(2)}, u32[]{:S(2)}) %collective-permute-start.2) | collective-permute-done | bytes 4194336 | tf_op jit(solution)/shard_map/ppermute | solution.py:21
  1145.2 163.7 %all-gather.31.cloned.1.call-done = bf16[2048,4096]{1,0:T(8,128)(2,1)} async-done(((bf16[512,4096]{1,0:T(8,128)(2,1)}), bf16[2048,4096]{1,0:T(8,128)(2,1)}) %all-gather.31.cloned.1.call-update) | async-done | bytes 16777232 | tf_op jit(solution)/shard_map/all_gather | solution.py:142
  1332.5 262.9 %all-gather.29.cloned.1.call-done = bf16[2048,4096]{1,0:T(8,128)(2,1)} async-done(((bf16[512,4096]{1,0:T(8,128)(2,1)}), bf16[2048,4096]{1,0:T(8,128)(2,1)}) %all-gather.29.cloned.1.call-update) | async-done | bytes 16777232 | tf_op jit(solution)/shard_map/all_gather | solution.py:141
  1595.4 57.0 %all-gather.27.cloned.1.call-done = bf16[1024,2048]{1,0:T(8,128)(2,1)} async-done(((bf16[512,2048]{1,0:T(8,128)(2,1)}), bf16[1024,2048]{1,0:T(8,128)(2,1)}) %all-gather.27.cloned.1.call-update) | async-done | bytes 4194320 | tf_op jit(solution)/shard_map/all_gather | solution.py:86
  1756.9 99.3 %reduce-scatter.20.cloned.1.call-done = f32[512,2048]{1,0:T(8,128)} async-done(((f32[1024,2048]{1,0:T(8,128)}), f32[512,2048]{1,0:T(8,128)}) %reduce-scatter.20.cloned.1.call-update) | async-done | bytes 4194320 | tf_op jit(solution)/shard_map/reduce_scatter | solution.py:90
  1865.0 56.6 %all-gather.35.cloned.1.call-done = bf16[1024,2048]{1,0:T(8,128)(2,1)} async-done(((bf16[512,2048]{1,0:T(8,128)(2,1)}), bf16[1024,2048]{1,0:T(8,128)(2,1)}) %all-gather.35.cloned.1.call-update) | async-done | bytes 4194320 | tf_op jit(solution)/shard_map/all_gather | solution.py:86
  1931.0 223.1 %while.52 = (s32[]{:T(128)}, f32[16,1024,1]{1,2,0:T(1,128)S(1)}, s32[4,1024]{1,0:T(4,128)S(1)}, s32[1024]{0:T(1024)S(1)}, s32[1024]{0:T(1024)S(1)}, /*index=5*/s...) while((s32[]{:T(128)}, f32[16,1024,1]{1,2,0:T(1,128)S(1)}, ...), condition=%wide.region_20.21_spmd.clone, body=%wide.region_18.20_spmd.clone.sunk | while | flops 4385163264 | bytes 145074336 | solution.py:247
  2154.1 522.8 %while.53 = (s32[]{:T(128)}, f32[1024,16,64]{0,2,1:T(8,128)}, bf16[4,1024,16,64]{1,3,2,0:T(8,128)(2,1)}, bf16[4,1024,16,64]{1,3,2,0:T(8,128)(2,1)}, bf16[4,1024,...) while((s32[]{:T(128)}, f32[1024,16,64]{0,2,1:T(8,128)}, ...), condition=%wide.region_22.23_spmd.clone, body=%wide.region_21.22_spmd.clone.sunk | while | flops 10915678208 | bytes 336832672 | solution.py:273
  2924.8 104.2 %reduce-scatter.40.cloned.1.call-done = bf16[128,4096]{1,0:T(8,128)(2,1)} async-done(((bf16[2048,4096]{1,0:T(8,128)(2,1)}), bf16[128,4096]{1,0:T(8,128)(2,1)}) %reduce-scatter.40.cloned.1.call-update) | async-done | bytes 1048592
  3032.2 178.3 %reduce-scatter.36.cloned.1.call-done = bf16[128,4096]{1,0:T(8,128)(2,1)} async-done(((bf16[2048,4096]{1,0:T(8,128)(2,1)}), bf16[128,4096]{1,0:T(8,128)(2,1)}) %reduce-scatter.36.cloned.1.call-update) | async-done | bytes 1048592 | tf_op jit(solution)/shard_map/reduce_scatter | solution.py:322
  3213.3 178.9 %reduce-scatter.38.cloned.1.call-done = bf16[128,4096]{1,0:T(8,128)(2,1)} async-done(((bf16[2048,4096]{1,0:T(8,128)(2,1)}), bf16[128,4096]{1,0:T(8,128)(2,1)}) %reduce-scatter.38.cloned.1.call-update) | async-done | bytes 1048592 | tf_op jit(solution)/shard_map/reduce_scatter | solution.py:325
  3395.0 72.6 %reduce-scatter.34.cloned.1.call-done = bf16[128,1024]{1,0:T(8,128)(2,1)} async-done(((bf16[2048,1024]{1,0:T(8,128)(2,1)}), bf16[128,1024]{1,0:T(8,128)(2,1)}) %reduce-scatter.34.cloned.1.call-update) | async-done | bytes 262160 | tf_op jit(solution)/shard_map/reduce_scatter | solution.py:319
  3469.4 74.4 %reduce-scatter.32.cloned.1.call-done = bf16[128,1024]{1,0:T(8,128)(2,1)} async-done(((bf16[2048,1024]{1,0:T(8,128)(2,1)}), bf16[128,1024]{1,0:T(8,128)(2,1)}) %reduce-scatter.32.cloned.1.call-update) | async-done | bytes 262160 | tf_op jit(solution)/shard_map/reduce_scatter | solution.py:316
  3545.5 73.6 %reduce-scatter.28.cloned.1.call-done = bf16[128,1024]{1,0:T(8,128)(2,1)} async-done(((bf16[2048,1024]{1,0:T(8,128)(2,1)}), bf16[128,1024]{1,0:T(8,128)(2,1)}) %reduce-scatter.28.cloned.1.call-update) | async-done | bytes 262160 | tf_op jit(solution)/shard_map/reduce_scatter | solution.py:310
  3621.0 74.4 %reduce-scatter.30.cloned.1.call-done = bf16[128,1024]{1,0:T(8,128)(2,1)} async-done(((bf16[2048,1024]{1,0:T(8,128)(2,1)}), bf16[128,1024]{1,0:T(8,128)(2,1)}) %reduce-scatter.30.cloned.1.call-update) | async-done | bytes 262160 | tf_op jit(solution)/shard_map/reduce_scatter | solution.py:313
  3697.1 98.6 %reduce-scatter.26.cloned.1.call-done = f32[512,2048]{1,0:T(8,128)} async-done(((f32[1024,2048]{1,0:T(8,128)}), f32[512,2048]{1,0:T(8,128)}) %reduce-scatter.26.cloned.1.call-update) | async-done | bytes 4194320 | tf_op jit(solution)/shard_map/reduce_scatter | solution.py:90
  3840.3 58.4 %reduce-scatter.18.cloned.1.call-done = f32[512,2048]{1,0:T(8,128)} async-done(((f32[1024,2048]{1,0:T(8,128)}), f32[512,2048]{1,0:T(8,128)}) %reduce-scatter.18.cloned.1.call-update) | async-done | bytes 4194320 | tf_op jit(solution)/shard_map/reduce_scatter | solution.py:90
  (379 shorter events, 1777.9 us)
Async XLA Ops:
  14.2 222.1 %all-gather.19.cloned.1.call-start = ((), (), s32[]{:S(2)}) async-start(), calls=%async_computation.16 | async-start | bytes 5242880 | tf_op jit(solution)/shard_map/all_gather | solution.py:135
  14.9 302.1 %all-gather.15.cloned.1.call-start = ((), (), s32[]{:S(2)}) async-start(), calls=%async_computation.14 | async-start | bytes 5242880 | tf_op jit(solution)/shard_map/all_gather | solution.py:136
  15.5 360.4 %all-gather.21.cloned.1.call-start = ((), (), s32[]{:S(2)}) async-start(), calls=%async_computation.17 | async-start | bytes 10485760 | tf_op jit(solution)/shard_map/all_gather | solution.py:154
  248.0 349.4 %all-gather.17.cloned.1.call-start = ((), (), s32[]{:S(2)}) async-start(), calls=%async_computation.15 | async-start | bytes 10485760 | tf_op jit(solution)/shard_map/all_gather | solution.py:155
  326.3 425.0 %all-gather.25.cloned.1.call-start = ((), (), s32[]{:S(2)}) async-start(), calls=%async_computation.19 | async-start | bytes 5242880 | tf_op jit(solution)/shard_map/all_gather | solution.py:137
  327.1 547.1 %reduce-scatter.16.cloned.1.call-start = ((), (), s32[]{:S(2)}) async-start(), calls=%async_computation.20 | async-start | bytes 12582912 | tf_op jit(solution)/shard_map/reduce_scatter | solution.py:90
  762.0 383.1 %all-gather.33.cloned.1.call-start = ((), (), s32[]{:S(2)}) async-start(), calls=%async_computation.25 | async-start | bytes 6291456 | tf_op jit(solution)/shard_map/all_gather | solution.py:86
  762.8 546.1 %all-gather.31.cloned.1.call-start = ((), (), s32[]{:S(2)}) async-start(), calls=%async_computation.23 | async-start | bytes 20971520 | tf_op jit(solution)/shard_map/all_gather | solution.py:142
  763.4 832.0 %all-gather.29.cloned.1.call-start = ((), (), s32[]{:S(2)}) async-start(), calls=%async_computation.22 | async-start | bytes 20971520 | tf_op jit(solution)/shard_map/all_gather | solution.py:141
  764.1 888.3 %all-gather.27.cloned.1.call-start = ((), (), s32[]{:S(2)}) async-start(), calls=%async_computation.21 | async-start | bytes 6291456 | tf_op jit(solution)/shard_map/all_gather | solution.py:86
  765.7 219.3 %collective-permute-start.1 = (bf16[512,4096]{1,0:T(8,128)(2,1)}, bf16[512,4096]{1,0:T(8,128)(2,1)}, u32[]{:S(2)}, u32[]{:S(2)}) collective-permute-start(bf16[512,4096]{1,0:T(8,128)(2,1)} %param.28), channel_id=1, source_target_pairs={{0,24},{8,0},{16,8},{24,16},{1,25},{9,1},{17,9},{25,17},{2,26},{10... | collective-permute-start | bytes 12582920 | tf_op jit(solution)/shard_map/ppermute | solution.py:24
  859.8 280.7 %collective-permute-start.2 = (bf16[512,4096]{1,0:T(8,128)(2,1)}, bf16[512,4096]{1,0:T(8,128)(2,1)}, u32[]{:S(2)}, u32[]{:S(2)}) collective-permute-start(bf16[512,4096]{1,0:T(8,128)(2,1)} %collective-permute-done), channel_id=1, source_target_pairs={{0,8},{8,16},{16,24},{24,0},{1,9},{9,17},{17,25},{25,1},{2,10},{10... | collective-permute-start | bytes 12582920 | tf_op jit(solution)/shard_map/ppermute | solution.py:21
  881.1 975.2 %reduce-scatter.20.cloned.1.call-start = ((), (), s32[]{:S(2)}) async-start(), calls=%async_computation.26 | async-start | bytes 12582912 | tf_op jit(solution)/shard_map/reduce_scatter | solution.py:90
  1756.9 164.7 %all-gather.35.cloned.1.call-start = ((), (), s32[]{:S(2)}) async-start(), calls=%async_computation.27 | async-start | bytes 6291456 | tf_op jit(solution)/shard_map/all_gather | solution.py:86
  1864.7 967.3 %reduce-scatter.24.cloned.1.call-start = ((), (), s32[]{:S(2)}) async-start(), calls=%async_computation.29 | async-start | bytes 10485760 | tf_op jit(solution)/shard_map/reduce_scatter | solution.py:283
  2725.2 303.8 %reduce-scatter.40.cloned.1.call-start = ((), (), s32[]{:S(2)}) async-start(), calls=%async_computation.37 | async-start | bytes 17825792
  2770.8 439.7 %reduce-scatter.36.cloned.1.call-start = ((), (), s32[]{:S(2)}) async-start(), calls=%async_computation.35 | async-start | bytes 17825792 | tf_op jit(solution)/shard_map/reduce_scatter | solution.py:322
  2795.9 596.3 %reduce-scatter.38.cloned.1.call-start = ((), (), s32[]{:S(2)}) async-start(), calls=%async_computation.36 | async-start | bytes 17825792 | tf_op jit(solution)/shard_map/reduce_scatter | solution.py:325
  2821.5 646.1 %reduce-scatter.34.cloned.1.call-start = ((), (), s32[]{:S(2)}) async-start(), calls=%async_computation.34 | async-start | bytes 4456448 | tf_op jit(solution)/shard_map/reduce_scatter | solution.py:319
  2831.7 712.0 %reduce-scatter.32.cloned.1.call-start = ((), (), s32[]{:S(2)}) async-start(), calls=%async_computation.33 | async-start | bytes 4456448 | tf_op jit(solution)/shard_map/reduce_scatter | solution.py:316
  2841.5 777.7 %reduce-scatter.28.cloned.1.call-start = ((), (), s32[]{:S(2)}) async-start(), calls=%async_computation.31 | async-start | bytes 4456448 | tf_op jit(solution)/shard_map/reduce_scatter | solution.py:310
  2860.1 835.3 %reduce-scatter.30.cloned.1.call-start = ((), (), s32[]{:S(2)}) async-start(), calls=%async_computation.32 | async-start | bytes 4456448 | tf_op jit(solution)/shard_map/reduce_scatter | solution.py:313
  2870.3 925.5 %reduce-scatter.26.cloned.1.call-start = ((), (), s32[]{:S(2)}) async-start(), calls=%async_computation.30 | async-start | bytes 12582912 | tf_op jit(solution)/shard_map/reduce_scatter | solution.py:90
  2900.3 998.3 %reduce-scatter.18.cloned.1.call-start = ((), (), s32[]{:S(2)}) async-start(), calls=%async_computation.24 | async-start | bytes 12582912 | tf_op jit(solution)/shard_map/reduce_scatter | solution.py:90
  (55 other events, 5863.1 us)
Sparse Core Ops, SparseCore 0:
  13.5 59.4 all-gather.12
  74.6 80.7 all-gather.22
  156.9 79.2 all-gather.18
  237.7 79.2 all-gather.14
  319.0 56.8 all-gather.20
  377.9 58.2 all-gather.16
  437.7 80.7 all-gather.24
  762.1 99.2 reduce-scatter.15
  863.1 56.7 all-gather.32
  921.3 387.5 all-gather.30
  1310.5 284.7 all-gather.28
  1757.0 99.2 reduce-scatter.19
  1864.8 56.7 all-gather.34
  2700.3 71.7 reduce-scatter.23
  2774.7 71.7 reduce-scatter.21
  2850.4 178.5 reduce-scatter.39
  3032.9 177.5 reduce-scatter.35
  3214.6 177.5 reduce-scatter.37
  3395.9 71.5 reduce-scatter.33
  3471.9 71.7 reduce-scatter.31
  3547.6 71.5 reduce-scatter.27
  3623.5 71.7 reduce-scatter.29
  3697.5 98.2 reduce-scatter.25
  3798.2 100.4 reduce-scatter.17
  (1 shorter events, 54.9 us)
